TPU v7x, 32 devices: a whole 2x2x4 slice. The times are simulated.
32 devices in a mesh: freq: 4 (over y, core), row: 4 (over z), col: 2 (over x).
Axes of the slice: x: 2, y: 2, z: 4, core: 2. Of those that a mesh axis runs over, the one named last changes fastest.
Arguments:
- voltages: bfloat16 [128, 259, 2048], P(('row', 'col', 'freq')), may hold values from -128 to 127, as said below
- tap_table: int32 [4, 2048], replicated, may hold values from -4096 to 4095
Outputs:
- visibility: float32 [1024, 2, 4, 32, 128], P('freq', None, None, 'col', 'row')
Inputs may be any that keep to these rules, and one draw needn't show every extreme that they name: `voltages`: whole numbers.
All inputs are finite; a program needn't handle non-finite values.
Results may differ from a plain program's by a relative error of at most 0.0033.
Values may be sent and summed in bfloat16 or wider, within the bound.
No kernel may reach another device: no remote copies, remote signals or barrier semaphores. Data moves between devices by JAX's collectives and lax.ppermute only.
A program may use at most 192 MiB of HBM per device.

v0:
```python
import math

import jax
import jax.numpy as jnp
from jax import lax
from jax.sharding import PartitionSpec as P


def dft_table(length, channels):
    sample = jnp.arange(length, dtype=jnp.int32)
    channel = jnp.arange(channels, dtype=jnp.int32)
    phase = channel[:, None] * sample[None, :] % length
    angle = phase.astype(jnp.float32) * (2.0 * math.pi / length)
    factor = 1.0 / (64.0 * math.sqrt(length))
    return jnp.stack([jnp.cos(angle) * factor, -jnp.sin(angle) * factor], axis=1)


def correlate(column_set, row_block):
    turned = jnp.concatenate([-column_set[:, 1:2], column_set[:, 0:1]], axis=1)
    stacked = jnp.concatenate([column_set, turned], axis=2)
    products = jnp.einsum("cpjt,cpit->cji", stacked, row_block, preferred_element_type=jnp.float32)
    column_count = column_set.shape[2]
    return jnp.stack([products[:, :column_count], products[:, column_count:]], axis=1)


def shards(voltages, tap_table):
    weights = tap_table.astype(jnp.float32) / 4096.0
    spec_count = voltages.shape[1] - tap_table.shape[0] + 1
    filtered = weights[0] * voltages[:, 0:spec_count, :].astype(jnp.float32)
    for tap_index in range(1, tap_table.shape[0]):
        filtered = filtered + weights[tap_index] * voltages[
            :, tap_index : tap_index + spec_count, :
        ].astype(jnp.float32)
    table = dft_table(voltages.shape[2], voltages.shape[2] // 2)
    spectra = jnp.einsum("cpn,isn->cpis", table, filtered, precision=lax.Precision.HIGHEST).astype(
        jnp.bfloat16
    )
    turned_block = lax.all_to_all(spectra, "freq", split_axis=0, concat_axis=2, tiled=True)
    channel_count = turned_block.shape[0]
    group_rows = turned_block.shape[2]
    row_block = lax.all_gather(turned_block, "col", axis=2, tiled=True)
    visibility = correlate(lax.all_gather(turned_block, "row", axis=2, tiled=True), row_block)
    visibility = visibility / spec_count
    return visibility.reshape(
        channel_count, 2, lax.axis_size("row"), group_rows, row_block.shape[2]
    )


def solution(mesh):
    in_specs = (P(("row", "col", "freq"), None, None), P())
    out_specs = P("freq", None, None, "col", "row")
    return jax.shard_map(shards, mesh=mesh, in_specs=in_specs, out_specs=out_specs, check_vma=False)
```

profile of v0, /device:TPU:0, one launch (start us, length us, event | category | flops | bytes accessed | tf_op | source)
XLA Modules:
  0.0 635.5 jit_solution(1949815385445334476)
XLA Ops:
  6.5 0.0 copy-start.1
  6.5 0.0 all-gather.3.cloned.1.call-start
  6.5 0.0 copy-start
  6.5 33.1 %negate_multiply_fusion = (f32[1024,1,2048]{2,0,1:T(8,128)S(1)}, f32[1024,1,2048]{2,0,1:T(8,128)S(1)}) fusion(), kind=kLoop, calls=%fused_computation.20 | loop fusion | flops 35651584 | bytes 16777216 | tf_op jit(solution)/shard_map/mul | solution.py:15
  39.7 0.0 copy-done.1
  39.7 0.0 copy-done
  39.7 10.2 %multiply_add_fusion = f32[4,256,2048]{2,0,1:T(4,128)} fusion(bf16[4,259,2048]{2,0,1:T(4,128)(2,1)S(1)} %copy-done, f32[2048]{0:T(1024)S(1)} %bitcast.34, f32[2048]{0:T(1024)S(1)} %bitcast.35, f32[2048]{0:T(1024)S(1)} %bitcast.36, f32[2048]{0:T(1024)S(1)} %bitcast.33), kind=kLoop, calls=%fused_computation.19 | loop fusion | flops 23068672 | bytes 25198592 | tf_op jit(solution)/shard_map/add | solution.py:31
  50.0 84.8 %fusion.17 = bf16[1024,2,4,256]{3,0,2,1:T(8,128)(2,1)S(1)} fusion(f32[4,256,2048]{2,0,1:T(4,128)} %multiply_add_fusion, f32[1024,1,2048]{2,0,1:T(8,128)S(1)} %get-tuple-element.13, f32[1024,1,2048]{2,0,1:T(8,128)S(1)} %get-tuple-element.14), kind=kOutput, calls=%fused_computation.27 | convolution fusion | flops 51545899008 | bytes 29360128 | tf_op jit(solution)/shard_map/cpn,isn->cpis/dot_general | solution.py:35
  134.8 3.2 copy.12
  138.0 52.2 %all_to_all.18 = bf16[1024,2,4,256]{3,2,1,0:T(4,128)(2,1)S(1)} all-to-all(bf16[1024,2,4,256]{3,2,1,0:T(4,128)(2,1)S(1)} %copy.12), channel_id=1, replica_groups=mesh['freq'=4,'row'=4,'col'=2] {'freq'}, dimensions={0} | all-to-all | bytes 8388608 | tf_op jit(solution)/shard_map/all_to_all | solution.py:38
  190.2 4.4 copy.26
  194.6 6.9 %all_to_all.16 = bf16[256,2,16,256]{3,2,1,0:T(8,128)(2,1)} reshape(bf16[256,2,4,4,256]{4,3,2,1,0:T(4,128)(2,1)} %bitcast.30) | data formatting | bytes 8388608 | tf_op jit(solution)/shard_map/all_to_all | solution.py:38
  201.5 0.0 all-gather.3.cloned.1.call-update
  201.6 0.0 all-gather.5.cloned.1.call-start
  201.6 0.7 all-gather.5.cloned.1.call-update
  202.3 286.5 %all-gather.3.cloned.1.call-done = bf16[256,2,64,256]{3,2,1,0:T(8,128)(2,1)} async-done(((bf16[256,2,16,256]{3,2,1,0:T(8,128)(2,1)}), bf16[256,2,64,256]{3,2,1,0:T(8,128)(2,1)}) %all-gather.3.cloned.1.call-update) | async-done | bytes 16777232 | tf_op jit(solution)/shard_map/all_gather | solution.py:42
  488.8 12.6 %slice_negate_fusion = (bf16[256,1,64,256]{3,2,1,0:T(8,128)(2,1)}, bf16[256,1,64,256]{3,2,1,0:T(8,128)(2,1)}) fusion(bf16[256,2,64,256]{3,2,1,0:T(8,128)(2,1)} %all-gather.3.cloned.1.call-done), kind=kLoop, calls=%fused_computation.16 | loop fusion | flops 4194304 | bytes 33554432 | tf_op jit(solution)/shard_map/neg | solution.py:19
  501.3 91.2 %all-gather.5.cloned.1.call-done = bf16[256,2,32,256]{3,2,1,0:T(8,128)(2,1)} async-done(((bf16[256,2,16,256]{3,2,1,0:T(8,128)(2,1)}), bf16[256,2,32,256]{3,2,1,0:T(8,128)(2,1)}) %all-gather.5.cloned.1.call-update) | async-done | bytes 8388624 | tf_op jit(solution)/shard_map/all_gather | solution.py:41
  592.5 17.1 %fusion.20 = f32[256,128,32]{1,2,0:T(8,128)S(1)} fusion(bf16[256,2,32,256]{3,2,1,0:T(8,128)(2,1)} %all-gather.5.cloned.1.call-done, bf16[256,1,64,256]{3,2,1,0:T(8,128)(2,1)} %get-tuple-element.6, bf16[256,1,64,256]{3,2,1,0:T(8,128)(2,1)} %get-tuple-element.5, bf16[256,2,64,256]{3,2,1,0:T(8,128)(2,1)} %all-gather.3.cloned.1.call-done), kind=kOutput, calls=%fused_computation.28 | convolution fusion | flops 1174405120 | bytes 46137344 | tf_op jit(solution)/shard_map/cpjt,cpit->cji/dot_general | solution.py:21
  609.6 4.9 fusion.25
  614.4 4.5 copy.14
  618.9 5.2 copy.15
  624.1 4.2 maximum_multiply_fusion
  (2 shorter events, 0.0 us)
Async XLA Ops:
  6.5 33.1 %copy-start.1 = (s32[4,2048]{1,0:T(4,128)S(1)}, s32[4,2048]{1,0:T(4,128)}, u32[]{:S(2)}) copy-start(s32[4,2048]{1,0:T(4,128)} %param.3) | copy-start | bytes 98308
  6.5 482.2 %all-gather.3.cloned.1.call-start = ((), (), s32[]{:S(2)}) async-start(), calls=%async_computation.1 | async-start | bytes 20971520 | tf_op jit(solution)/shard_map/all_gather | solution.py:42
  6.5 33.2 %copy-start = (bf16[4,259,2048]{2,0,1:T(4,128)(2,1)S(1)}, bf16[4,259,2048]{2,0,1:T(4,128)(2,1)}, u32[]{:S(2)}) copy-start(bf16[4,259,2048]{2,0,1:T(4,128)(2,1)} %param.2) | copy-start | bytes 12730372
  201.6 390.9 %all-gather.5.cloned.1.call-start = ((), (), s32[]{:S(2)}) async-start(), calls=%async_computation.2 | async-start | bytes 12582912 | tf_op jit(solution)/shard_map/all_gather | solution.py:41
Sparse Core Ops, SparseCore 0:
  201.7 287.0 all-gather.2
  490.3 102.1 all-gather.4
where the time goes:
time: 642 us; the launch traced here: 636 us
  waiting for transfers between devices  378 us (59%)
  matrix products  102 us (16%)
  other arithmetic  60.2 us (9%)
  blocking collectives  52.2 us (8%)
  local copies, waits for them, and re-layouts  29.1 us (5%)
  between operations  13.8 us (2%)
    all_gather x1, waiting for transfers between devices, shards(): lax.all_gather(turned_block, 'row', axis=2, tiled=True)  286 us
    all_gather x1, waiting for transfers between devices, shards(): row_block = lax.all_gather(turned_block, 'col', axis=2, tiled=True)  91.2 us
    dot_general x1, matrix products, shards(): jnp.einsum('cpn,isn->cpis', table, filtered, precision=lax.Precision.HIGH...  84.8 us
    all_to_all x1, blocking collectives, shards(): lax.all_to_all(spectra, 'freq', split_axis=0, concat_axis=2, tiled=True)  52.2 us
    mul x1, other arithmetic, dft_table(): -jnp.sin(angle) * factor  33.1 us
    dot_general x1, matrix products, correlate(): jnp.einsum('cpjt,cpit->cji', stacked, row_block, preferred_element_type=j...  17.1 us
  transfers between devices with their start and end apart: 2, of which 2 were waited for; matrix products, arithmetic and copies ran while one was open for 2% of the time, Pallas kernels for 0%

commit v1 on v0

v1 whole, which is shorter than its diff:
```python
import functools
import math

import jax
import jax.numpy as jnp
import numpy as np
from jax import lax
from jax.experimental import pallas as pl
from jax.experimental.pallas import tpu as pltpu
from jax.sharding import PartitionSpec as P

OWNERS = ("col", "row")
EVERYONE = ("col", "row", "freq")


def split(value):
    high = value.astype(jnp.bfloat16)
    low = (value - high.astype(jnp.float32)).astype(jnp.bfloat16)
    return high, low


def dft_tables(length, channels, parity, groups):
    half = length // 2
    stride = 2 ** ((channels.bit_length() - 1) // 2)
    sample = np.arange(half)
    coarse = 2.0 * math.pi / length * ((np.arange(0, channels, stride)[:, None] * sample) % length)
    fine = 2.0 * math.pi / length * ((np.arange(parity, stride, 2)[:, None] * sample) % length)
    factor = 1.0 / (64.0 * math.sqrt(length))
    cos_a, sin_a = (jnp.asarray((f(coarse) * factor)[:, None], jnp.float32) for f in (np.cos, np.sin))
    cos_b, sin_b = (jnp.asarray(f(fine)[None], jnp.float32) for f in (np.cos, np.sin))
    real = (cos_a * cos_b - sin_a * sin_b).reshape(groups, -1, half)
    imag = (-(sin_a * cos_b) - cos_a * sin_b).reshape(groups, -1, half)
    return split(jnp.stack([real, imag], axis=1).reshape(groups, -1, half))


def dft_kernel(owners, table_high, table_low, data_high, data_low, out):
    dims = (((1,), (1,)), ((), ()))
    dot = functools.partial(lax.dot_general, dimension_numbers=dims, preferred_element_type=jnp.float32)
    high, low = table_high[0], table_low[0]
    result = dot(high, data_high[...]) + (dot(high, data_low[...]) + dot(low, data_high[...]))
    result = result.astype(jnp.bfloat16)
    count = out.shape[3]
    for part in range(2):
        for owner in range(owners):
            start = (part * owners + owner) * count
            out[owner, 0, part] = result[start : start + count]


def dft(tables, data, groups, owners):
    table_high, table_low = tables
    data_high, data_low = data
    rows, half = table_high.shape[1:]
    width = data_high.shape[0]
    count = rows // 2 // owners
    table_spec = pl.BlockSpec((1, rows, half), lambda g: (g, 0, 0))
    data_spec = pl.BlockSpec((width, half), lambda g: (0, 0))
    return pl.pallas_call(
        functools.partial(dft_kernel, owners),
        grid=(groups,),
        in_specs=[table_spec, table_spec, data_spec, data_spec],
        out_specs=pl.BlockSpec((owners, 1, 2, count, width), lambda g: (0, g, 0, 0, 0)),
        out_shape=jax.ShapeDtypeStruct((owners, groups, 2, count, width), jnp.bfloat16),
        cost_estimate=pl.CostEstimate(
            flops=6 * groups * rows * half * width,
            bytes_accessed=4 * (groups * rows * half + width * half) + 2 * groups * rows * width,
            transcendentals=0,
        ),
    )(table_high, table_low, data_high, data_low)


def shards(voltages, tap_table):
    groups, row_count, col_count = (lax.axis_size(name) for name in ("freq", "row", "col"))
    owners = row_count * col_count
    inputs, frames, length = voltages.shape
    taps = tap_table.shape[0]
    spec_count = frames - taps + 1
    channels, half = length // 2, length // 2
    weights = tap_table.astype(jnp.float32) / 4096.0
    filtered = weights[0] * voltages[:, 0:spec_count, :].astype(jnp.float32)
    for k in range(1, taps):
        filtered = filtered + weights[k] * voltages[:, k : k + spec_count, :].astype(jnp.float32)
    first, second = filtered[..., :half], filtered[..., half:]
    sent = []
    for parity, folded in enumerate((first + second, first - second)):
        data = split(folded.reshape(inputs * spec_count, half))
        sent.append(dft(dft_tables(length, channels, parity, groups), data, groups, owners))
    sent = jnp.stack(sent, axis=4)
    count = sent.shape[3]
    got = lax.all_to_all(
        sent.reshape(owners * groups, 2, 2 * count, inputs * spec_count), EVERYONE, split_axis=0, concat_axis=0, tiled=True
    )
    got = got.reshape(col_count, row_count, groups, 2, 2 * count, inputs, spec_count)
    got = got.transpose(4, 3, 1, 0, 2, 5, 6).reshape(2 * count, 2, -1, spec_count)
    turned = jnp.stack([-got[:, 1], got[:, 0]], axis=1)
    stacked = jnp.concatenate([got, turned], axis=2)
    products = jnp.einsum("cpjt,cpit->cji", stacked, got, preferred_element_type=jnp.float32) / spec_count
    block = groups * inputs
    products = products.astype(jnp.bfloat16).reshape(2 * count, 2, row_count, col_count, block, row_count, col_count * block)
    products = products.transpose(3, 5, 0, 1, 2, 4, 6).reshape(owners, 2 * count, 2, row_count * block, col_count * block)
    back = lax.all_to_all(products, OWNERS, split_axis=0, concat_axis=0, tiled=True)
    back = back.reshape(owners * 2 * count, 2, row_count, block, col_count * block)
    return back.astype(jnp.float32)


def solution(mesh):
    in_specs = (P(("row", "col", "freq"), None, None), P())
    out_specs = P("freq", None, None, "col", "row")
    return jax.shard_map(shards, mesh=mesh, in_specs=in_specs, out_specs=out_specs, check_vma=False)
```

time: 642 us -> 315 us (0.49)
  waiting for transfers between devices: 378 us -> 0 us
  blocking collectives: 52.2 us -> 154 us
  matrix products: 102 us -> 6.99 us
  local copies, waits for them, and re-layouts: 29.1 us -> 96.6 us
  other arithmetic: 60.2 us -> 34 us
  Pallas kernels: 0 us -> 21.7 us
  between operations: 13.8 us -> 0.16 us
    all_gather x2 -> x0, waiting for transfers between devices: 378 us -> none  [the longest x1 286 us: shards(): lax.all_gather(turned_block, 'row', axis=2, tiled=True)]
    all_to_all x1 -> x2, blocking collectives: 52.2 us -> 154 us  [the longest x1 102 us: shards(): lax.all_to_all(sent.reshape(owners * groups, 2, 2 * count, inputs * spec_...]
    dot_general x2 -> x1, matrix products: 102 us -> 6.99 us  [shards(): jnp.einsum('cpjt,cpit->cji', stacked, got, preferred_element_type=jnp.flo...]
    reshape x0 -> x5, local copies, waits for them, and re-layouts: none -> 38 us  [the longest x2 15 us: shards(): products.astype(jnp.bfloat16)]
    mul x1 -> x0, other arithmetic: 33.1 us -> none  [dft_table(): -jnp.sin(angle) * factor]
    convert_element_type x1 -> x2, local copies, waits for them, and re-layouts: 3.24 us -> 27 us  [shards(): return back.astype(jnp.float32)]
    pallas_call x0 -> x2, Pallas kernels: none -> 21.7 us  [dft(): pl.pallas_call(functools.partial(dft_kernel, owners), grid=(groups,), in_...]
    slice x3 -> x0, local copies, waits for them, and re-layouts: 14.5 us -> none  [the longest x2 9.33 us: correlate(): products[:, :column_count]]
  transfers between devices with their start and end apart: 2 -> 0, of which waited for: 2 -> 0; matrix products, arithmetic and copies ran while one was open for 2% -> 0% of each run, Pallas kernels for 0% -> 0%
where the time goes in v1:
time: 315 us; the launch traced here: 314 us
  blocking collectives  154 us (49%)
  local copies, waits for them, and re-layouts  96.6 us (31%)
  other arithmetic  34 us (11%)
  Pallas kernels  21.7 us (7%)
  matrix products  6.99 us (2%)
    all_to_all x1, blocking collectives, shards(): lax.all_to_all(sent.reshape(owners * groups, 2, 2 * count, inputs * spec_...  102 us
    all_to_all x1, blocking collectives, shards(): lax.all_to_all(products, OWNERS, split_axis=0, concat_axis=0, tiled=True)  52.3 us
    convert_element_type x2, local copies, waits for them, and re-layouts, shards(): return back.astype(jnp.float32)  27 us
    pallas_call x2, Pallas kernels, dft(): pl.pallas_call(functools.partial(dft_kernel, owners), grid=(groups,), in_...  21.7 us
    reshape x2, local copies, waits for them, and re-layouts, shards(): products.astype(jnp.bfloat16)  15 us
    unnamed x16, local copies, waits for them, and re-layouts  13.8 us
    convert_element_type x4, other arithmetic, split(): low = (value - high.astype(jnp.float32)).astype(jnp.bfloat16)  11.4 us
    add x1, other arithmetic, shards(): filtered + weights[k] * voltages[:, k:k + spec_count, :].astype(jnp.float32)  10.4 us

profile of v1, /device:TPU:0, one launch (start us, length us, event | category | flops | bytes accessed | tf_op | source)
XLA Modules:
  0.0 313.9 jit_solution(4282235544380034503)
XLA Ops:
  0.8 10.4 %multiply_add_fusion = f32[4,256,2048]{2,0,1:T(4,128)S(1)} fusion(bf16[4,259,2048]{2,0,1:T(4,128)(2,1)} %param.10, f32[2048]{0:T(1024)S(1)} %bitcast.66, f32[2048]{0:T(1024)S(1)} %bitcast.67, f32[2048]{0:T(1024)S(1)} %bitcast.68, f32[2048]{0:T(1024)S(1)} %bitcast.65), kind=kLoop, calls=%fused_computation.6 | loop fusion | flops 23068672 | bytes 25198592 | tf_op jit(solution)/shard_map/add | solution.py:81
  11.2 2.6 slice_add_fusion
  13.7 2.4 copy.20
  16.2 2.8 fusion.9
  21.5 2.8 fusion.7
  26.3 2.8 fusion.10
  29.7 2.9 fusion.8
  32.6 10.8 %shard_map.100 = bf16[8,4,2,16,1024]{4,3,2,1,0:T(8,128)(2,1)} custom-call(bf16[4,256,1024]{2,1,0:T(8,128)(2,1)} %get-tuple-element.8.table_high, bf16[4,256,1024]{2,1,0:T(8,128)(2,1)} %get-tuple-element.7.table_low, bf16[1024,1024]{1,0:T(8,128)(2,1)} %get-tuple-element.6.data_high, bf16[1024,1024]{1,0:T(8,128)(2,1)} %get-tuple-element.5.data_low), custom_call_target="tpu_custom_call" | custom-call | flops 6442450944 | bytes 10485760 | tf_op jit(solution)/shard_map/pallas_call | solution.py:57
  43.4 10.9 %shard_map.101 = bf16[8,4,2,16,1024]{4,3,2,1,0:T(8,128)(2,1)} custom-call(bf16[4,256,1024]{2,1,0:T(8,128)(2,1)} %get-tuple-element.12.table_high, bf16[4,256,1024]{2,1,0:T(8,128)(2,1)} %get-tuple-element.11.table_low, bf16[1024,1024]{1,0:T(8,128)(2,1)} %get-tuple-element.10.data_high, bf16[1024,1024]{1,0:T(8,128)(2,1)} %get-tuple-element.9.data_low), custom_call_target="tpu_custom_call" | custom-call | flops 6442450944 | bytes 10485760 | tf_op jit(solution)/shard_map/pallas_call | solution.py:57
  56.3 6.4 %copy.22 = bf16[8,4,2,16,2,1024]{5,2,4,3,1,0:T(2,128)(2,1)} copy(bf16[8,4,2,16,2,1024]{5,3,2,1,0,4:T(8,128)(2,1)S(1)} %pad_maximum_fusion.2) | data formatting | bytes 8388608 | tf_op jit(solution)/shard_map/stack | solution.py:87
  62.7 102.1 %all_to_all.10 = bf16[32,2,32,1024]{3,1,2,0:T(2,128)(2,1)} all-to-all(bf16[32,2,32,1024]{3,1,2,0:T(2,128)(2,1)} %bitcast.57), channel_id=1, replica_groups=mesh['freq'=4,'row'=4,'col'=2] {'col','row','freq'}, dimensions={0} | all-to-all | bytes 8388608 | tf_op jit(solution)/shard_map/all_to_all | solution.py:89
  164.8 7.6 %reshape.213 = bf16[2,4,4,2,32,4,256]{6,5,3,4,2,1,0:T(4,128)(2,1)} reshape(bf16[32,2,32,1024]{3,1,2,0:T(2,128)(2,1)} %all_to_all.10) | data formatting | bytes 8388608 | tf_op jit(solution)/shard_map/reshape | solution.py:92
  172.4 6.5 %copy.24 = bf16[32,2,4,2,4,4,256]{6,5,4,3,2,1,0:T(4,128)(2,1)} copy(bf16[32,2,4,2,4,4,256]{6,5,1,0,4,2,3:T(4,128)(2,1)} %bitcast.58) | data formatting | bytes 8388608 | tf_op jit(solution)/shard_map/transpose | solution.py:93
  178.9 6.9 %reshape.208 = bf16[32,2,128,256]{3,2,1,0:T(8,128)(2,1)} reshape(bf16[32,2,4,2,4,4,256]{6,5,4,3,2,1,0:T(4,128)(2,1)} %copy.24) | data formatting | bytes 8388608 | tf_op jit(solution)/shard_map/reshape | solution.py:93
  185.8 4.5 %slice_negate_fusion = (bf16[32,1,128,256]{3,2,1,0:T(8,128)(2,1)}, bf16[32,1,128,256]{3,2,1,0:T(8,128)(2,1)}) fusion(bf16[32,2,128,256]{3,2,1,0:T(8,128)(2,1)} %reshape.208), kind=kLoop, calls=%fused_computation.26 | loop fusion | flops 1048576 | bytes 8388608 | tf_op jit(solution)/shard_map/neg | solution.py:94
  190.3 7.0 %fusion.6 = bf16[32,256,128]{2,1,0:T(8,128)(2,1)S(1)} fusion(bf16[32,2,128,256]{3,2,1,0:T(8,128)(2,1)} %reshape.208, bf16[32,1,128,256]{3,2,1,0:T(8,128)(2,1)} %get-tuple-element.16, bf16[32,1,128,256]{3,2,1,0:T(8,128)(2,1)} %get-tuple-element.15), kind=kOutput, calls=%fused_computation.11 | convolution fusion | flops 1101004800 | bytes 10485760 | tf_op jit(solution)/shard_map/cpjt,cpit->cji/dot_general | solution.py:96
  197.3 6.1 %reshape.209 = bf16[32,2,4,2,16,4,32]{6,5,4,3,2,1,0:T(4,128)(2,1)} reshape(bf16[32,256,128]{2,1,0:T(8,128)(2,1)S(1)} %fusion.6) | data formatting | bytes 4194304 | tf_op jit(solution)/shard_map/reshape | solution.py:98
  203.4 8.9 %copy.25 = bf16[32,2,4,2,16,4,32]{6,4,2,1,0,5,3:T(8,128)(2,1)} copy(bf16[32,2,4,2,16,4,32]{6,5,4,3,2,1,0:T(4,128)(2,1)} %reshape.209) | data formatting | bytes 4194304 | tf_op jit(solution)/shard_map/reshape | solution.py:98
  212.3 8.5 %copy.26 = bf16[8,32,2,64,32]{3,4,2,1,0:T(8,128)(2,1)} copy(bf16[8,32,2,64,32]{4,3,2,1,0:T(8,128)(2,1)} %bitcast.54) | data formatting | bytes 4194304 | tf_op jit(solution)/shard_map/reshape | solution.py:99
  220.8 6.4 %reshape.214 = bf16[8,2,65536]{2,1,0:T(2,128)(2,1)S(1)} reshape(bf16[8,32,2,32,64]{4,3,2,1,0:T(8,128)(2,1)} %bitcast.55) | data formatting | bytes 4194304
  227.2 52.3 %all_to_all.11 = bf16[8,2,65536]{2,1,0:T(2,128)(2,1)} all-to-all(bf16[8,2,65536]{2,1,0:T(2,128)(2,1)S(1)} %reshape.214), channel_id=1, replica_groups=mesh['freq'=4,'row'=4,'col'=2] {'col','row'}, dimensions={0} | all-to-all | bytes 4194304 | tf_op jit(solution)/shard_map/all_to_all | solution.py:100
  279.5 7.4 %reshape.215 = bf16[8,32,2,32,64]{4,3,2,1,0:T(8,128)(2,1)} reshape(bf16[8,2,65536]{2,1,0:T(2,128)(2,1)} %all_to_all.11) | data formatting | bytes 4194304
  286.9 14.8 %copy.27 = f32[8,32,2,64,32]{1,0,4,3,2:T(8,128)} copy(bf16[8,32,2,64,32]{3,4,2,1,0:T(8,128)(2,1)} %bitcast.56) | data formatting | bytes 6291456 | tf_op jit(solution)/shard_map/convert_element_type | solution.py:102
  301.7 12.2 %reshape.211 = f32[256,2,4,16,32]{0,4,3,2,1:T(8,128)} reshape(f32[8,32,2,64,32]{1,0,4,3,2:T(8,128)} %copy.27) | data formatting | bytes 8388608 | tf_op jit(solution)/shard_map/convert_element_type | solution.py:102
  (21 shorter events, 7.7 us)
Async XLA Ops:
  21.4 2.9 copy-start.1
  21.5 2.9 copy-start.2
  21.5 2.9 copy-start.3
  21.5 2.9 copy-start.4
  21.5 2.9 copy-start.5
  21.5 2.9 copy-start.6
  43.4 10.9 %copy-start = (bf16[8,4,2,16,1024]{4,3,2,1,0:T(8,128)(2,1)S(1)}, bf16[8,4,2,16,1024]{4,3,2,1,0:T(8,128)(2,1)}, u32[]{:S(2)}) copy-start(bf16[8,4,2,16,1024]{4,3,2,1,0:T(8,128)(2,1)} %shard_map.100) | copy-start | bytes 6291460

commit v2 on v1

v2 whole, which is shorter than its diff:
```python
import functools
import math

import jax
import jax.numpy as jnp
import numpy as np
from jax import lax
from jax.experimental import pallas as pl
from jax.experimental.pallas import tpu as pltpu
from jax.sharding import PartitionSpec as P

OWNERS = ("col", "row")
EVERYONE = ("col", "row", "freq")
ROWS_ALIKE = (((1,), (1,)), ((), ()))
WHOLE = pl.BlockSpec(memory_space=pltpu.VMEM)


def split(value):
    high = value.astype(jnp.bfloat16)
    low = (value - high.astype(jnp.float32)).astype(jnp.bfloat16)
    return high, low


def dft_tables(length, channels, parity, groups):
    half = length // 2
    stride = 2 ** ((channels.bit_length() - 1) // 2)
    sample = np.arange(half)
    factor = 1.0 / (64.0 * math.sqrt(length))
    coarse = 2.0 * math.pi / length * ((np.arange(0, channels, stride)[:, None] * sample) % length)
    fine = 2.0 * math.pi / length * ((np.arange(parity, stride, 2)[:, None] * sample) % length)
    coarse = np.stack([np.cos(coarse), np.sin(coarse)], axis=1) * factor
    fine = np.stack([np.cos(fine), np.sin(fine)])
    return jnp.asarray(coarse.reshape(groups, -1, half), jnp.float32), jnp.asarray(fine, jnp.float32)


def dft_kernel(parity, owners, volts, taps, coarse, fine, out, fold, high, low, table_high, table_low):
    frames, inputs, length = volts.shape
    half = length // 2
    tap_count = taps.shape[0]
    spec_count = frames - tap_count + 1
    step, lanes = 8, 128
    rows = step * inputs

    @pl.when(pl.program_id(0) == 0)
    def _():
        for start in range(0, half, lanes):
            pair = (start, start + half)
            weights = [taps[:, pl.ds(at, lanes)].astype(jnp.float32) / 4096.0 for at in pair]

            def filter_rows(index, carry):
                total = None
                for at, weight in zip(pair, weights):
                    block = volts[pl.ds(index * step, step + tap_count - 1), :, pl.ds(at, lanes)].astype(jnp.float32)
                    block = block.reshape(-1, lanes)
                    value = weight[0:1] * block[:rows]
                    for k in range(1, tap_count):
                        value = value + weight[k : k + 1] * block[k * inputs : k * inputs + rows]
                    total = value if total is None else (total - value if parity else total + value)
                fold[pl.ds(pl.multiple_of(index * rows, rows), rows), :] = total
                return carry

            lax.fori_loop(0, spec_count // step, filter_rows, 0)
            for i in range(inputs):
                high_part, low_part = split(fold[pl.ds(i, spec_count, stride=inputs), :])
                high[pl.ds(i * spec_count, spec_count), pl.ds(start, lanes)] = high_part
                low[pl.ds(i * spec_count, spec_count), pl.ds(start, lanes)] = low_part

    fine_count = fine.shape[1]
    group_rows = table_high.shape[0] // 2
    for a in range(group_rows // fine_count):
        cos_a, sin_a = coarse[0, 2 * a : 2 * a + 1], coarse[0, 2 * a + 1 : 2 * a + 2]
        real = cos_a * fine[0] - sin_a * fine[1]
        imag = -(sin_a * fine[0]) - cos_a * fine[1]
        for part, value in enumerate((real, imag)):
            at = pl.ds(part * group_rows + a * fine_count, fine_count)
            table_high[at], table_low[at] = split(value)

    dot = functools.partial(lax.dot_general, dimension_numbers=ROWS_ALIKE, preferred_element_type=jnp.float32)
    result = dot(table_high[...], high[...]) + (dot(table_high[...], low[...]) + dot(table_low[...], high[...]))
    result = result.astype(jnp.bfloat16)
    count = out.shape[3]
    for part in range(2):
        for owner in range(owners):
            start = (part * owners + owner) * count
            out[owner, 0, part] = result[start : start + count]


def dft(volts, taps, parity, groups, owners):
    frames, inputs, length = volts.shape
    spec_count = frames - taps.shape[0] + 1
    half = length // 2
    coarse, fine = dft_tables(length, half, parity, groups)
    count = half // 2 // groups // owners
    width = inputs * spec_count
    group_rows = half // 2 // groups
    return pl.pallas_call(
        functools.partial(dft_kernel, parity, owners),
        grid=(groups,),
        in_specs=[WHOLE, WHOLE, pl.BlockSpec((1,) + coarse.shape[1:], lambda g: (g, 0, 0)), WHOLE],
        out_specs=pl.BlockSpec((owners, 1, 2, count, width), lambda g: (0, g, 0, 0, 0)),
        out_shape=jax.ShapeDtypeStruct((owners, groups, 2, count, width), jnp.bfloat16),
        scratch_shapes=[
            pltpu.VMEM((width, 128), jnp.float32),
            pltpu.VMEM((width, half), jnp.bfloat16),
            pltpu.VMEM((width, half), jnp.bfloat16),
            pltpu.VMEM((2 * group_rows, half), jnp.bfloat16),
            pltpu.VMEM((2 * group_rows, half), jnp.bfloat16),
        ],
        cost_estimate=pl.CostEstimate(
            flops=6 * half * half * width, bytes_accessed=2 * frames * inputs * length + 2 * half * width, transcendentals=0
        ),
    )(volts, taps, coarse, fine)


def correlate_kernel(sizes, got, out, scratch):
    cols, rows, groups, inputs = sizes
    sources, _, count, width = got.shape
    spec_count = width // inputs
    tiles = width // 128
    for part in range(2):
        for tile in range(tiles):
            value = got[:, part, :, tile * 128 : (tile + 1) * 128].astype(jnp.float32)
            scratch[part * tiles + tile] = value.reshape(sources * count, 128)

    def one_channel(k, carry):
        loaded = [scratch[x, pl.ds(k, sources, stride=count), :].astype(jnp.bfloat16) for x in range(2 * tiles)]
        each = tiles // inputs
        parts = [jnp.concatenate(loaded[x * each : (x + 1) * each], axis=1) for x in range(2 * inputs)]
        real, imag = parts[:inputs], parts[inputs:]
        left = jnp.concatenate([jnp.concatenate(x, axis=0) for x in (real, imag)], axis=1)
        near, far = [], []
        for col in range(cols):
            at = slice(col * rows * groups, (col + 1) * rows * groups)
            near += [x[at] for x in real] + [-x[at] for x in imag]
            far += [x[at] for x in imag] + [x[at] for x in real]
        right = jnp.concatenate([jnp.concatenate(near, axis=0), jnp.concatenate(far, axis=0)], axis=1)
        value = lax.dot_general(left, right, ROWS_ALIKE, preferred_element_type=jnp.float32) * (1.0 / spec_count)
        lanes = value.shape[1] // cols
        for row in range(rows):
            picked = jnp.concatenate(
                [value[(x * rows + row) * groups : (x * rows + row + 1) * groups] for x in range(inputs * cols)], axis=0
            ).astype(jnp.bfloat16)
            for col in range(cols):
                out[col * rows + row, k] = picked[:, col * lanes : (col + 1) * lanes]
        return carry

    lax.fori_loop(0, count, one_channel, 0)


def correlate(got, sizes):
    cols, rows, groups, inputs = sizes
    sources, _, count, width = got.shape
    block = groups * inputs
    shape = (cols * rows, count, cols * block, 2 * rows * block)
    return pl.pallas_call(
        functools.partial(correlate_kernel, sizes),
        in_specs=[WHOLE],
        out_specs=WHOLE,
        out_shape=jax.ShapeDtypeStruct(shape, jnp.bfloat16),
        scratch_shapes=[pltpu.VMEM((2 * width // 128, sources * count, 128), jnp.float32)],
        cost_estimate=pl.CostEstimate(
            flops=8 * count * sources * inputs * sources * width,
            bytes_accessed=2 * math.prod(got.shape) + 2 * math.prod(shape),
            transcendentals=0,
        ),
    )(got)


def finish_kernel(sizes, even, odd, place, out, scratch, held, sem):
    cols, rows, groups, inputs = sizes
    owners, count, width, lanes = even.shape
    tiles = lanes // 128
    for parity, got in enumerate((even, odd)):
        for tile in range(tiles):
            value = got[:, :, :, tile * 128 : (tile + 1) * 128].astype(jnp.float32)
            scratch[parity * tiles + tile] = value.reshape(owners * count * width, 128)

    def one_row(x, carry):
        i, rest = x // (cols * groups), x % (cols * groups)
        at = rest * inputs + i
        values = []
        for tile in range(tiles):
            pair = [scratch[p * tiles + tile, pl.ds(x, owners * count, stride=width), :] for p in range(2)]
            values.append(jnp.concatenate(pair, axis=0).T.astype(jnp.bfloat16))
        value = jnp.dot(jnp.concatenate(values, axis=0), place[...], preferred_element_type=jnp.float32)
        for part in range(2):
            for j in range(inputs):
                start = (part * inputs + j) * rows * groups
                first = part * rows * groups * inputs * width + j * width + at
                for half in range(held.shape[0]):
                    piece = value[start : start + rows * groups, half * 128 : (half + 1) * 128]
                    held[half, pl.ds(first, rows * groups, stride=inputs * width), :] = piece
        return carry

    lax.fori_loop(0, width, one_row, 0)
    copies = [
        pltpu.make_async_copy(held.at[half], out.at[:, pl.ds(half * 128, 128)], sem.at[half])
        for half in range(held.shape[0])
    ]
    for copy in copies:
        copy.start()
    for copy in copies:
        copy.wait()


def finish(even, odd, sizes):
    cols, rows, groups, inputs = sizes
    owners, count, width, lanes = even.shape
    channels = 2 * owners * count
    if channels % 128:
        value = jnp.stack([even, odd], axis=2).astype(jnp.float32)
        value = value.reshape(channels, inputs, cols, groups, 2, inputs, rows, groups)
        return value.transpose(4, 6, 7, 5, 2, 3, 1, 0).reshape(lanes * width, channels)
    source = np.arange(channels)
    target = source % (channels // 2) * 2 + source // (channels // 2)
    place = jnp.asarray(np.eye(channels)[target], jnp.bfloat16)
    return pl.pallas_call(
        functools.partial(finish_kernel, sizes),
        in_specs=[WHOLE] * 3,
        out_specs=pl.BlockSpec(memory_space=pl.ANY),
        out_shape=jax.ShapeDtypeStruct((lanes * width, channels), jnp.float32),
        scratch_shapes=[
            pltpu.VMEM((2 * lanes // 128, owners * count * width, 128), jnp.float32),
            pltpu.VMEM((channels // 128, lanes * width, 128), jnp.float32),
            pltpu.SemaphoreType.DMA((channels // 128,)),
        ],
    )(even, odd, place)


def shards(voltages, tap_table):
    groups, rows, cols = (lax.axis_size(name) for name in ("freq", "row", "col"))
    inputs = voltages.shape[0]
    sizes = (cols, rows, groups, inputs)
    volts = voltages.transpose(1, 0, 2)
    back = []
    for parity in range(2):
        sent = dft(volts, tap_table, parity, groups, rows * cols)
        sent = sent.reshape((-1,) + sent.shape[2:])
        got = lax.all_to_all(sent, EVERYONE, split_axis=0, concat_axis=0, tiled=True)
        back.append(lax.all_to_all(correlate(got, sizes), OWNERS, split_axis=0, concat_axis=0, tiled=True))
    result = finish(*back, sizes)
    block = groups * inputs
    return result.reshape(2, rows, block, cols * block, -1).transpose(4, 0, 1, 2, 3)


def solution(mesh):
    in_specs = (P(("row", "col", "freq"), None, None), P())
    out_specs = P("freq", None, None, "col", "row")
    return jax.shard_map(shards, mesh=mesh, in_specs=in_specs, out_specs=out_specs, check_vma=False)
```

time: 315 us -> 208 us (0.66)
  blocking collectives: 154 us -> 29.7 us
  local copies, waits for them, and re-layouts: 96.6 us -> 1.32 us
  waiting for transfers between devices: 0 us -> 93.6 us
  Pallas kernels: 21.7 us -> 68.1 us
  other arithmetic: 34 us -> 0 us
  starting transfers between devices: 0 us -> 14.4 us
  matrix products: 6.99 us -> 0 us
    all_to_all x2 -> x1, blocking collectives: 154 us -> 29.7 us  [shards(): lax.all_to_all(correlate(got, sizes), OWNERS, split_axis=0, concat_axis=0...]
    all_to_all x0 -> x3, waiting for transfers between devices: none -> 93.6 us  [the longest x2 75 us: shards(): lax.all_to_all(sent, EVERYONE, split_axis=0, concat_axis=0, tiled=True)]
    pallas_call x2 -> x5, Pallas kernels: 21.7 us -> 68.1 us  [the longest x2 34.5 us: dft(): pl.pallas_call(functools.partial(dft_kernel, parity, owners), grid=(group...]
    reshape x5 -> x0, local copies, waits for them, and re-layouts: 38 us -> none  [the longest x2 15 us: shards(): products.astype(jnp.bfloat16)]
    convert_element_type x2 -> x0, local copies, waits for them, and re-layouts: 27 us -> none  [shards(): return back.astype(jnp.float32)]
    all_to_all x0 -> x3, starting transfers between devices: none -> 14.4 us  [the longest x2 10.8 us: shards(): lax.all_to_all(sent, EVERYONE, split_axis=0, concat_axis=0, tiled=True)]
    add x2 -> x0, other arithmetic: 12.9 us -> none  [the longest x1 10.4 us: shards(): filtered + weights[k] * voltages[:, k:k + spec_count, :].astype(jnp.float32)]
    unnamed x16 -> x4, local copies, waits for them, and re-layouts: 13.8 us -> 1.32 us
  transfers between devices with their start and end apart: 0 -> 3, of which waited for: 0 -> 3; matrix products, arithmetic and copies ran while one was open for 0% -> 0% of each run, Pallas kernels for 0% -> 16%
where the time goes in v2:
time: 208 us; the launch traced here: 207 us
  waiting for transfers between devices  93.6 us (45%)
  Pallas kernels  68.1 us (33%)
  blocking collectives  29.7 us (14%)
  starting transfers between devices  14.4 us (7%)
    all_to_all x2, waiting for transfers between devices, shards(): lax.all_to_all(sent, EVERYONE, split_axis=0, concat_axis=0, tiled=True)  75 us
    pallas_call x2, Pallas kernels, dft(): pl.pallas_call(functools.partial(dft_kernel, parity, owners), grid=(group...  34.5 us
    all_to_all x1, blocking collectives, shards(): lax.all_to_all(correlate(got, sizes), OWNERS, split_axis=0, concat_axis=0...  29.7 us
    all_to_all x1, waiting for transfers between devices, shards(): lax.all_to_all(correlate(got, sizes), OWNERS, split_axis=0, concat_axis=0...  18.6 us
    pallas_call x1, Pallas kernels, finish(): pl.pallas_call(functools.partial(finish_kernel, sizes), in_specs=[WHOLE]...  17.7 us
    pallas_call x2, Pallas kernels, correlate(): pl.pallas_call(functools.partial(correlate_kernel, sizes), in_specs=[WHOL...  15.8 us
    all_to_all x2, starting transfers between devices, shards(): lax.all_to_all(sent, EVERYONE, split_axis=0, concat_axis=0, tiled=True)  10.8 us
  transfers between devices with their start and end apart: 3, of which 3 were waited for; matrix products, arithmetic and copies ran while one was open for 0% of the time, Pallas kernels for 16%

profile of v2, /device:TPU:0, one launch (start us, length us, event | category | flops | bytes accessed | tf_op | source)
XLA Modules:
  0.0 207.1 jit_solution(17183333052510971034)
XLA Ops:
  0.0 17.3 %shard_map.73 = bf16[8,4,2,16,1024]{4,3,2,1,0:T(8,128)(2,1)} custom-call(bf16[259,4,2048]{2,1,0:T(4,128)(2,1)} %bitcast.8, s32[4,2048]{1,0:T(4,128)} %taps.3, f32[4,16,1024]{2,1,0:T(8,128)} %constant.8.clone.coarse, f32[2,16,1024]{2,1,0:T(8,128)} %constant.9.clone.fine), custom_call_target="tpu_custom_call" | custom-call | flops 6442450944 | bytes 6340608 | tf_op jit(solution)/shard_map/pallas_call | solution.py:96
  17.3 7.3 %all-to-all-start = ((bf16[32,2,16,1024]{3,2,1,0:T(8,128)(2,1)}), bf16[32,2,16,1024]{3,2,1,0:T(8,128)(2,1)S(1)}, u32[]{:S(2)}, u32[]{:S(2)}) async-start(bf16[32,2,16,1024]{3,2,1,0:T(8,128)(2,1)} %bitcast.7), calls=%async_computation | async-start | bytes 4194304 | tf_op jit(solution)/shard_map/all_to_all | solution.py:239
  24.6 17.3 %shard_map.75 = bf16[8,4,2,16,1024]{4,3,2,1,0:T(8,128)(2,1)} custom-call(bf16[259,4,2048]{2,1,0:T(4,128)(2,1)} %bitcast.9, s32[4,2048]{1,0:T(4,128)} %taps.3, f32[4,16,1024]{2,1,0:T(8,128)} %constant.8.clone.coarse, f32[2,16,1024]{2,1,0:T(8,128)} %constant.10.clone.fine), custom_call_target="tpu_custom_call" | custom-call | flops 6442450944 | bytes 6340608 | tf_op jit(solution)/shard_map/pallas_call | solution.py:96
  41.9 32.8 %all-to-all-done.got = bf16[32,2,16,1024]{3,2,1,0:T(8,128)(2,1)S(1)} async-done(((bf16[32,2,16,1024]{3,2,1,0:T(8,128)(2,1)}), bf16[32,2,16,1024]{3,2,1,0:T(8,128)(2,1)S(1)}, u32[]{:S(2)}, u32[]{:S(2)}) %all-to-all-start) | async-done | bytes 2097184 | tf_op jit(solution)/shard_map/all_to_all | solution.py:239
  74.7 0.0 copy-start
  74.7 1.3 copy-done
  76.0 3.5 %all-to-all-start.2 = ((bf16[32,2,16,1024]{3,2,1,0:T(8,128)(2,1)}), bf16[32,2,16,1024]{3,2,1,0:T(8,128)(2,1)}, u32[]{:S(2)}, u32[]{:S(2)}) async-start(bf16[32,2,16,1024]{3,2,1,0:T(8,128)(2,1)} %bitcast.6), calls=%async_computation.2 | async-start | bytes 4194304 | tf_op jit(solution)/shard_map/all_to_all | solution.py:239
  79.5 7.9 %shard_map.74 = bf16[8,16,32,128]{3,2,1,0:T(8,128)(2,1)} custom-call(bf16[32,2,16,1024]{3,2,1,0:T(8,128)(2,1)} %copy-done), custom_call_target="tpu_custom_call" | custom-call | flops 536870912 | bytes 3145728 | tf_op jit(solution)/shard_map/pallas_call | solution.py:155
  87.4 42.2 %all-to-all-done.2.got = bf16[32,2,16,1024]{3,2,1,0:T(8,128)(2,1)} async-done(((bf16[32,2,16,1024]{3,2,1,0:T(8,128)(2,1)}), bf16[32,2,16,1024]{3,2,1,0:T(8,128)(2,1)}, u32[]{:S(2)}, u32[]{:S(2)}) %all-to-all-start.2) | async-done | bytes 2097184 | tf_op jit(solution)/shard_map/all_to_all | solution.py:239
  129.6 3.6 %all-to-all-start.1 = ((bf16[8,16,32,128]{3,2,1,0:T(8,128)(2,1)}), bf16[8,16,32,128]{3,2,1,0:T(8,128)(2,1)S(1)}, u32[]{:S(2)}, u32[]{:S(2)}) async-start(bf16[8,16,32,128]{3,2,1,0:T(8,128)(2,1)} %shard_map.74), calls=%async_computation.1 | async-start | bytes 2097152 | tf_op jit(solution)/shard_map/all_to_all | solution.py:240
  133.1 7.9 %shard_map.76 = bf16[8,16,32,128]{3,2,1,0:T(8,128)(2,1)} custom-call(bf16[32,2,16,1024]{3,2,1,0:T(8,128)(2,1)} %all-to-all-done.2.got), custom_call_target="tpu_custom_call" | custom-call | flops 536870912 | bytes 3145728 | tf_op jit(solution)/shard_map/pallas_call | solution.py:155
  141.1 18.6 %all-to-all-done.1.even = bf16[8,16,32,128]{3,2,1,0:T(8,128)(2,1)S(1)} async-done(((bf16[8,16,32,128]{3,2,1,0:T(8,128)(2,1)}), bf16[8,16,32,128]{3,2,1,0:T(8,128)(2,1)S(1)}, u32[]{:S(2)}, u32[]{:S(2)}) %all-to-all-start.1) | async-done | bytes 1048608 | tf_op jit(solution)/shard_map/all_to_all | solution.py:240
  159.7 0.0 copy-start.1
  159.7 29.7 %all_to_all.20.odd = bf16[8,16,32,128]{3,2,1,0:T(8,128)(2,1)} all-to-all(bf16[8,16,32,128]{3,2,1,0:T(8,128)(2,1)} %shard_map.76), channel_id=1, replica_groups=mesh['freq'=4,'row'=4,'col'=2] {'col','row'}, dimensions={0} | all-to-all | bytes 2097152 | tf_op jit(solution)/shard_map/all_to_all | solution.py:240
  189.4 0.0 copy-done.1
  189.4 17.7 %shard_map.77 = f32[4096,256]{1,0:T(8,128)} custom-call(bf16[8,16,32,128]{3,2,1,0:T(8,128)(2,1)} %copy-done.1, bf16[8,16,32,128]{3,2,1,0:T(8,128)(2,1)} %all_to_all.20.odd, bf16[256,256]{1,0:T(8,128)(2,1)} %constant.11.clone.place), custom_call_target="tpu_custom_call" | custom-call | tf_op jit(solution)/shard_map/pallas_call | solution.py:217
Async XLA Ops:
  17.3 57.4 %all-to-all-start = ((bf16[32,2,16,1024]{3,2,1,0:T(8,128)(2,1)}), bf16[32,2,16,1024]{3,2,1,0:T(8,128)(2,1)S(1)}, u32[]{:S(2)}, u32[]{:S(2)}) async-start(bf16[32,2,16,1024]{3,2,1,0:T(8,128)(2,1)} %bitcast.7), calls=%async_computation | async-start | bytes 4194304 | tf_op jit(solution)/shard_map/all_to_all | solution.py:239
  74.7 1.3 copy-start
  76.0 53.6 %all-to-all-start.2 = ((bf16[32,2,16,1024]{3,2,1,0:T(8,128)(2,1)}), bf16[32,2,16,1024]{3,2,1,0:T(8,128)(2,1)}, u32[]{:S(2)}, u32[]{:S(2)}) async-start(bf16[32,2,16,1024]{3,2,1,0:T(8,128)(2,1)} %bitcast.6), calls=%async_computation.2 | async-start | bytes 4194304 | tf_op jit(solution)/shard_map/all_to_all | solution.py:239
  129.6 30.1 %all-to-all-start.1 = ((bf16[8,16,32,128]{3,2,1,0:T(8,128)(2,1)}), bf16[8,16,32,128]{3,2,1,0:T(8,128)(2,1)S(1)}, u32[]{:S(2)}, u32[]{:S(2)}) async-start(bf16[8,16,32,128]{3,2,1,0:T(8,128)(2,1)} %shard_map.74), calls=%async_computation.1 | async-start | bytes 2097152 | tf_op jit(solution)/shard_map/all_to_all | solution.py:240
  159.7 29.7 %copy-start.1 = (bf16[8,16,32,128]{3,2,1,0:T(8,128)(2,1)}, bf16[8,16,32,128]{3,2,1,0:T(8,128)(2,1)S(1)}, u32[]{:S(2)}) copy-start(bf16[8,16,32,128]{3,2,1,0:T(8,128)(2,1)S(1)} %all-to-all-done.1.even) | copy-start | bytes 3145732

commit v3 on v2

v3 whole, which is shorter than its diff:
```python
import functools
import math

import jax
import jax.numpy as jnp
import numpy as np
from jax import lax
from jax.experimental import pallas as pl
from jax.experimental.pallas import tpu as pltpu
from jax.sharding import PartitionSpec as P

OWNERS = ("col", "row")
EVERYONE = ("col", "row", "freq")
ROWS_ALIKE = (((1,), (1,)), ((), ()))
WHOLE = pl.BlockSpec(memory_space=pltpu.VMEM)

FOURS = (0, 4, ((1, 1, 1, 1),))
TWOS = (2, 4, ((1, -1, 1, -1),))
ODDS = (1, 2, ((1, 0, -1, 0), (0, 1, 0, -1)))
CHUNKS = ((FOURS,), (TWOS, ODDS))


def split(value):
    high = value.astype(jnp.bfloat16)
    low = (value - high.astype(jnp.float32)).astype(jnp.bfloat16)
    return high, low


def angle_tables(length, channels, kind):
    residue, modulus, folds = kind
    stride = 2 ** ((channels.bit_length() - 1) // 2)
    sample = np.arange(length // 4 * len(folds))
    factor = 1.0 / (64.0 * math.sqrt(length))
    coarse = 2.0 * math.pi / length * ((np.arange(0, channels, stride)[:, None] * sample) % length)
    fine = 2.0 * math.pi / length * ((np.arange(residue, stride, modulus)[:, None] * sample) % length)
    coarse = np.stack([np.cos(coarse), np.sin(coarse)]) * factor
    fine = np.stack([np.cos(fine), np.sin(fine)])
    return jnp.asarray(coarse, jnp.float32), jnp.asarray(fine, jnp.float32)


def signed_sum(values, signs):
    total = None
    for value, sign in zip(values, signs):
        if sign:
            total = value * sign if total is None else (total + value if sign > 0 else total - value)
    return total


def dft_kernel(kinds, volts, taps, *refs):
    tables, out, scratch = refs[: 2 * len(kinds)], refs[2 * len(kinds)], refs[2 * len(kinds) + 1 :]
    fold, scratch = scratch[0], scratch[1:]
    frames, inputs, length = volts.shape
    quarter = length // 4
    tap_count = taps.shape[0]
    spec_count = frames - tap_count + 1
    step, lanes = 8, 128
    rows = step * inputs
    for start in range(0, quarter, lanes):
        starts = [start + x * quarter for x in range(4)]
        weights = [taps[:, pl.ds(at, lanes)].astype(jnp.float32) / 4096.0 for at in starts]

        def filter_rows(index, carry):
            values = []
            for at, weight in zip(starts, weights):
                block = volts[pl.ds(index * step, step + tap_count - 1), :, pl.ds(at, lanes)].astype(jnp.float32)
                block = block.reshape(-1, lanes)
                value = weight[0:1] * block[:rows]
                for k in range(1, tap_count):
                    value = value + weight[k : k + 1] * block[k * inputs : k * inputs + rows]
                values.append(value)
            piece = 0
            for _, _, folds in kinds:
                for signs in folds:
                    fold[piece, pl.ds(pl.multiple_of(index * rows, rows), rows), :] = signed_sum(values, signs)
                    piece += 1
            return carry

        lax.fori_loop(0, spec_count // step, filter_rows, 0)
        piece = 0
        for x, (_, _, folds) in enumerate(kinds):
            high, low = scratch[4 * x : 4 * x + 2]
            for y in range(len(folds)):
                for i in range(inputs):
                    at = pl.ds(i * spec_count, spec_count), pl.ds(y * quarter + start, lanes)
                    high[at], low[at] = split(fold[piece, pl.ds(i, spec_count, stride=inputs), :])
                piece += 1

    dot = functools.partial(lax.dot_general, dimension_numbers=ROWS_ALIKE, preferred_element_type=jnp.float32)
    owners, groups, _, count, _ = out.shape
    slot = 0
    for x in range(len(kinds)):
        coarse, fine = tables[2 * x : 2 * x + 2]
        high, low, table_high, table_low = scratch[4 * x : 4 * x + 4]
        channels = table_high.shape[0] // 2
        fine_count = fine.shape[1]
        for a in range(channels // fine_count):
            cos_a, sin_a = coarse[0, a : a + 1], coarse[1, a : a + 1]
            real = cos_a * fine[0] - sin_a * fine[1]
            imag = -(sin_a * fine[0]) - cos_a * fine[1]
            for part, value in enumerate((real, imag)):
                at = pl.ds(part * channels + a * fine_count, fine_count)
                table_high[at], table_low[at] = split(value)
        result = dot(table_high[...], high[...]) + (dot(table_high[...], low[...]) + dot(table_low[...], high[...]))
        result = result.astype(jnp.bfloat16)
        each = channels // groups // owners
        for part in range(2):
            for group in range(groups):
                for owner in range(owners):
                    start = ((part * groups + group) * owners + owner) * each
                    out[owner, group, part, slot : slot + each] = result[start : start + each]
        slot += each


def dft(volts, taps, kinds, groups, owners):
    frames, inputs, length = volts.shape
    width = inputs * (frames - taps.shape[0] + 1)
    channels = length // 2
    operands, scratch, count, pieces, flops = [volts, taps], [], 0, 0, 0
    for kind in kinds:
        _, modulus, folds = kind
        operands += angle_tables(length, channels, kind)
        folded, rows = length // 4 * len(folds), 2 * channels // modulus
        scratch += [pltpu.VMEM((width, folded), jnp.bfloat16)] * 2 + [pltpu.VMEM((rows, folded), jnp.bfloat16)] * 2
        count += channels // modulus // groups // owners
        pieces += len(folds)
        flops += 6 * rows * folded * width
    shape = (owners, groups, 2, count, width)
    return pl.pallas_call(
        functools.partial(dft_kernel, kinds),
        in_specs=[WHOLE] * len(operands),
        out_specs=WHOLE,
        out_shape=jax.ShapeDtypeStruct(shape, jnp.bfloat16),
        scratch_shapes=[pltpu.VMEM((pieces, width, 128), jnp.float32)] + scratch,
        cost_estimate=pl.CostEstimate(
            flops=flops, bytes_accessed=2 * frames * inputs * length + 2 * math.prod(shape), transcendentals=0
        ),
    )(*operands)


def correlate_kernel(sizes, got, out, scratch):
    cols, rows, groups, inputs = sizes
    sources, _, count, width = got.shape
    spec_count = width // inputs
    tiles = width // 128
    for part in range(2):
        for tile in range(tiles):
            value = got[:, part, :, tile * 128 : (tile + 1) * 128].astype(jnp.float32)
            scratch[part * tiles + tile] = value.reshape(sources * count, 128)

    def one_channel(k, carry):
        loaded = [scratch[x, pl.ds(k, sources, stride=count), :].astype(jnp.bfloat16) for x in range(2 * tiles)]
        each = tiles // inputs
        parts = [jnp.concatenate(loaded[x * each : (x + 1) * each], axis=1) for x in range(2 * inputs)]
        real, imag = parts[:inputs], parts[inputs:]
        left = jnp.concatenate([jnp.concatenate(x, axis=0) for x in (real, imag)], axis=1)
        near, far = [], []
        for col in range(cols):
            at = slice(col * rows * groups, (col + 1) * rows * groups)
            near += [x[at] for x in real] + [-x[at] for x in imag]
            far += [x[at] for x in imag] + [x[at] for x in real]
        right = jnp.concatenate([jnp.concatenate(near, axis=0), jnp.concatenate(far, axis=0)], axis=1)
        value = lax.dot_general(left, right, ROWS_ALIKE, preferred_element_type=jnp.float32) * (1.0 / spec_count)
        lanes = value.shape[1] // cols
        for row in range(rows):
            picked = jnp.concatenate(
                [value[(x * rows + row) * groups : (x * rows + row + 1) * groups] for x in range(inputs * cols)], axis=0
            ).astype(jnp.bfloat16)
            for col in range(cols):
                out[col * rows + row, k] = picked[:, col * lanes : (col + 1) * lanes]
        return carry

    lax.fori_loop(0, count, one_channel, 0, unroll=2)


def correlate(got, sizes):
    cols, rows, groups, inputs = sizes
    sources, _, count, width = got.shape
    block = groups * inputs
    shape = (cols * rows, count, cols * block, 2 * rows * block)
    return pl.pallas_call(
        functools.partial(correlate_kernel, sizes),
        in_specs=[WHOLE],
        out_specs=WHOLE,
        out_shape=jax.ShapeDtypeStruct(shape, jnp.bfloat16),
        scratch_shapes=[pltpu.VMEM((2 * width // 128, sources * count, 128), jnp.float32)],
        cost_estimate=pl.CostEstimate(
            flops=8 * count * sources * inputs * sources * width,
            bytes_accessed=2 * math.prod(got.shape) + 2 * math.prod(shape),
            transcendentals=0,
        ),
    )(got)


def places(count_of):
    result = []
    for kinds in CHUNKS:
        result.append([residue + modulus * x for residue, modulus, _ in kinds for x in range(count_of(modulus))])
    return result


def finish_kernel(sizes, *refs):
    chunks, (same, out, scratch, held, sem) = refs[: len(CHUNKS)], refs[len(CHUNKS) :]
    cols, rows, groups, inputs = sizes
    owners, _, width, lanes = chunks[0].shape
    total = sum(got.shape[1] for got in chunks)
    tiles = lanes // 128
    for got, slots in zip(chunks, places(lambda modulus: total // modulus)):
        for owner in range(owners):
            for slot, place in enumerate(slots):
                for tile in range(tiles):
                    value = got[owner, slot, :, tile * 128 : (tile + 1) * 128].astype(jnp.float32)
                    scratch[tile, pl.ds((owner * total + place) * width, width), :] = value

    def one_row(x, carry):
        i, rest = x // (cols * groups), x % (cols * groups)
        at = rest * inputs + i
        for tile in range(tiles):
            block = scratch[tile, pl.ds(x, owners * total, stride=width), :].astype(jnp.bfloat16)
            value = lax.dot_general(same[...], block, ROWS_ALIKE, preferred_element_type=jnp.float32)
            for y in range(128 // (rows * groups)):
                first = (tile * (128 // (rows * groups)) + y)
                start = (first // inputs * rows * groups * inputs + first % inputs) * width + at
                for half in range(held.shape[0]):
                    piece = value[y * rows * groups : (y + 1) * rows * groups, half * 128 : (half + 1) * 128]
                    held[half, pl.ds(start, rows * groups, stride=inputs * width), :] = piece
        return carry

    lax.fori_loop(0, width, one_row, 0, unroll=4)
    copies = [
        pltpu.make_async_copy(held.at[half], out.at[:, pl.ds(half * 128, 128)], sem.at[half])
        for half in range(held.shape[0])
    ]
    for copy in copies:
        copy.start()
    for copy in copies:
        copy.wait()


def finish(chunks, sizes):
    cols, rows, groups, inputs = sizes
    owners, _, width, lanes = chunks[0].shape
    total = sum(got.shape[1] for got in chunks)
    channels = owners * total
    if channels % 128 or 128 % (rows * groups):
        order = np.argsort(sum(places(lambda modulus: total // modulus), []))
        value = jnp.concatenate(chunks, axis=1)[:, order].astype(jnp.float32)
        value = value.reshape(channels, inputs, cols, groups, 2, inputs, rows, groups)
        return value.transpose(4, 6, 7, 5, 2, 3, 1, 0).reshape(lanes * width, channels)
    return pl.pallas_call(
        functools.partial(finish_kernel, sizes),
        in_specs=[WHOLE] * (len(chunks) + 1),
        out_specs=pl.BlockSpec(memory_space=pl.ANY),
        out_shape=jax.ShapeDtypeStruct((lanes * width, channels), jnp.float32),
        scratch_shapes=[
            pltpu.VMEM((lanes // 128, channels * width, 128), jnp.float32),
            pltpu.VMEM((channels // 128, lanes * width, 128), jnp.float32),
            pltpu.SemaphoreType.DMA((channels // 128,)),
        ],
    )(*chunks, jnp.eye(128, dtype=jnp.bfloat16))


def shards(voltages, tap_table):
    groups, rows, cols = (lax.axis_size(name) for name in ("freq", "row", "col"))
    inputs = voltages.shape[0]
    sizes = (cols, rows, groups, inputs)
    volts = voltages.transpose(1, 0, 2)
    back = []
    for kinds in CHUNKS:
        sent = dft(volts, tap_table, kinds, groups, rows * cols)
        sent = sent.reshape((-1,) + sent.shape[2:])
        got = lax.all_to_all(sent, EVERYONE, split_axis=0, concat_axis=0, tiled=True)
        back.append(lax.all_to_all(correlate(got, sizes), OWNERS, split_axis=0, concat_axis=0, tiled=True))
    result = finish(back, sizes)
    block = groups * inputs
    return result.reshape(2, rows, block, cols * block, -1).transpose(4, 0, 1, 2, 3)


def solution(mesh):
    in_specs = (P(("row", "col", "freq"), None, None), P())
    out_specs = P("freq", None, None, "col", "row")
    return jax.shard_map(shards, mesh=mesh, in_specs=in_specs, out_specs=out_specs, check_vma=False)
```

time: 208 us -> 193 us (0.928)
  blocking collectives: 29.7 us -> 0 us
  waiting for transfers between devices: 93.6 us -> 122 us
  Pallas kernels: 68.1 us -> 50 us
  starting transfers between devices: 14.4 us -> 17.8 us
    all_to_all x1 -> x0, blocking collectives: 29.7 us -> none  [shards(): lax.all_to_all(correlate(got, sizes), OWNERS, split_axis=0, concat_axis=0...]
    all_to_all x1 -> x2, waiting for transfers between devices: 18.6 us -> 43.9 us  [shards(): lax.all_to_all(correlate(got, sizes), OWNERS, split_axis=0, concat_axis=0...]
    pallas_call x1, Pallas kernels: 17.7 us -> 10.6 us  [finish(): pl.pallas_call(functools.partial(finish_kernel, sizes), in_specs=[WHOLE]...]
    pallas_call x2, Pallas kernels: 34.5 us -> 28.4 us  [dft(): pl.pallas_call(functools.partial(dft_kernel, kinds), in_specs=[WHOLE] * l...]
    pallas_call x2, Pallas kernels: 15.8 us -> 11 us  [correlate(): pl.pallas_call(functools.partial(correlate_kernel, sizes), in_specs=[WHOL...]
    all_to_all x1 -> x2, starting transfers between devices: 3.56 us -> 7.73 us  [shards(): lax.all_to_all(correlate(got, sizes), OWNERS, split_axis=0, concat_axis=0...]
    all_to_all x2, waiting for transfers between devices: 75 us -> 77.7 us  [shards(): lax.all_to_all(sent, EVERYONE, split_axis=0, concat_axis=0, tiled=True)]
  transfers between devices with their start and end apart: 3 -> 4, of which waited for: 3 -> 4; matrix products, arithmetic and copies ran while one was open for 0% -> 0% of each run, Pallas kernels for 16% -> 15%
where the time goes in v3:
time: 193 us; the launch traced here: 192 us
  waiting for transfers between devices  122 us (63%)
  Pallas kernels  50 us (26%)
  starting transfers between devices  17.8 us (9%)
  local copies, waits for them, and re-layouts  2.13 us (1%)
    all_to_all x2, waiting for transfers between devices, shards(): lax.all_to_all(sent, EVERYONE, split_axis=0, concat_axis=0, tiled=True)  77.7 us
    all_to_all x2, waiting for transfers between devices, shards(): lax.all_to_all(correlate(got, sizes), OWNERS, split_axis=0, concat_axis=0...  43.9 us
    pallas_call x2, Pallas kernels, dft(): pl.pallas_call(functools.partial(dft_kernel, kinds), in_specs=[WHOLE] * l...  28.4 us
    pallas_call x2, Pallas kernels, correlate(): pl.pallas_call(functools.partial(correlate_kernel, sizes), in_specs=[WHOL...  11 us
    pallas_call x1, Pallas kernels, finish(): pl.pallas_call(functools.partial(finish_kernel, sizes), in_specs=[WHOLE]...  10.6 us
    all_to_all x2, starting transfers between devices, shards(): lax.all_to_all(sent, EVERYONE, split_axis=0, concat_axis=0, tiled=True)  10.1 us
    all_to_all x2, starting transfers between devices, shards(): lax.all_to_all(correlate(got, sizes), OWNERS, split_axis=0, concat_axis=0...  7.73 us
  transfers between devices with their start and end apart: 4, of which 4 were waited for; matrix products, arithmetic and copies ran while one was open for 0% of the time, Pallas kernels for 15%

profile of v3, /device:TPU:0, one launch (start us, length us, event | category | flops | bytes accessed | tf_op | source)
XLA Modules:
  0.0 192.2 jit_solution(2291251575609048613)
XLA Ops:
  0.0 9.9 %shard_map.82 = bf16[8,4,2,8,1024]{4,3,2,1,0:T(8,128)(2,1)} custom-call(bf16[259,4,2048]{2,1,0:T(4,128)(2,1)} %bitcast.8, s32[4,2048]{1,0:T(4,128)} %taps.3, f32[2,32,512]{2,1,0:T(8,128)} %constant.10.clone.refs_0_, f32[2,8,512]{2,1,0:T(8,128)} %constant.11.clone.refs_1_), custom_call_target="tpu_custom_call" | custom-call | flops 1610612736 | bytes 5292032 | tf_op jit(solution)/shard_map/pallas_call | solution.py:128
  9.9 7.3 %all-to-all-start = ((bf16[32,2,8,1024]{3,2,1,0:T(8,128)(2,1)}), bf16[32,2,8,1024]{3,2,1,0:T(8,128)(2,1)S(1)}, u32[]{:S(2)}, u32[]{:S(2)}) async-start(bf16[32,2,8,1024]{3,2,1,0:T(8,128)(2,1)} %bitcast.7), calls=%async_computation | async-start | bytes 2097152 | tf_op jit(solution)/shard_map/all_to_all | solution.py:271
  17.2 18.5 %shard_map.84 = bf16[8,4,2,24,1024]{4,3,2,1,0:T(8,128)(2,1)} custom-call(bf16[259,4,2048]{2,1,0:T(4,128)(2,1)} %bitcast.9, s32[4,2048]{1,0:T(4,128)} %taps.3, f32[2,32,512]{2,1,0:T(8,128)} %constant.10.clone.refs_0_, f32[2,8,512]{2,1,0:T(8,128)} %constant.12.clone.refs_1_, f32[2,32,1024]{2,1,0:T(8,128)} %constant.13.clone.refs_2_, ...), custom_call_target="tpu_custom_call" | custom-call | flops 8053063680 | bytes 7389184 | tf_op jit(solution)/shard_map/pallas_call | solution.py:128
  35.7 8.6 %all-to-all-done.got = bf16[32,2,8,1024]{3,2,1,0:T(8,128)(2,1)S(1)} async-done(((bf16[32,2,8,1024]{3,2,1,0:T(8,128)(2,1)}), bf16[32,2,8,1024]{3,2,1,0:T(8,128)(2,1)S(1)}, u32[]{:S(2)}, u32[]{:S(2)}) %all-to-all-start) | async-done | bytes 1048608 | tf_op jit(solution)/shard_map/all_to_all | solution.py:271
  44.4 0.0 copy-start.2
  44.4 1.0 copy-done.2
  45.4 2.8 %all-to-all-start.2 = ((bf16[32,2,24,1024]{3,2,1,0:T(8,128)(2,1)}), bf16[32,2,24,1024]{3,2,1,0:T(8,128)(2,1)S(1)}, u32[]{:S(2)}, u32[]{:S(2)}) async-start(bf16[32,2,24,1024]{3,2,1,0:T(8,128)(2,1)} %bitcast.6), calls=%async_computation.2 | async-start | bytes 6291456 | tf_op jit(solution)/shard_map/all_to_all | solution.py:271
  48.2 3.5 %shard_map.83 = bf16[8,8,32,128]{3,2,1,0:T(8,128)(2,1)} custom-call(bf16[32,2,8,1024]{3,2,1,0:T(8,128)(2,1)} %copy-done.2), custom_call_target="tpu_custom_call" | custom-call | flops 268435456 | bytes 1572864 | tf_op jit(solution)/shard_map/pallas_call | solution.py:180
  51.7 69.0 %all-to-all-done.2.got = bf16[32,2,24,1024]{3,2,1,0:T(8,128)(2,1)S(1)} async-done(((bf16[32,2,24,1024]{3,2,1,0:T(8,128)(2,1)}), bf16[32,2,24,1024]{3,2,1,0:T(8,128)(2,1)S(1)}, u32[]{:S(2)}, u32[]{:S(2)}) %all-to-all-start.2) | async-done | bytes 3145760 | tf_op jit(solution)/shard_map/all_to_all | solution.py:271
  120.7 0.0 copy-start
  120.7 4.1 %all-to-all-start.1 = ((bf16[8,8,32,128]{3,2,1,0:T(8,128)(2,1)}), bf16[8,8,32,128]{3,2,1,0:T(8,128)(2,1)}, u32[]{:S(2)}, u32[]{:S(2)}) async-start(bf16[8,8,32,128]{3,2,1,0:T(8,128)(2,1)} %shard_map.83), calls=%async_computation.1 | async-start | bytes 1048576 | tf_op jit(solution)/shard_map/all_to_all | solution.py:272
  124.9 0.0 copy-done
  124.9 7.5 %shard_map.85 = bf16[8,24,32,128]{3,2,1,0:T(8,128)(2,1)} custom-call(bf16[32,2,24,1024]{3,2,1,0:T(8,128)(2,1)} %copy-done), custom_call_target="tpu_custom_call" | custom-call | flops 805306368 | bytes 4718592 | tf_op jit(solution)/shard_map/pallas_call | solution.py:180
  132.4 7.9 %all-to-all-done.1.refs_0_ = bf16[8,8,32,128]{3,2,1,0:T(8,128)(2,1)} async-done(((bf16[8,8,32,128]{3,2,1,0:T(8,128)(2,1)}), bf16[8,8,32,128]{3,2,1,0:T(8,128)(2,1)}, u32[]{:S(2)}, u32[]{:S(2)}) %all-to-all-start.1) | async-done | bytes 524320 | tf_op jit(solution)/shard_map/all_to_all | solution.py:272
  140.2 3.6 %all-to-all-start.3 = ((bf16[8,24,32,128]{3,2,1,0:T(8,128)(2,1)}), bf16[8,24,32,128]{3,2,1,0:T(8,128)(2,1)S(1)}, u32[]{:S(2)}, u32[]{:S(2)}) async-start(bf16[8,24,32,128]{3,2,1,0:T(8,128)(2,1)} %shard_map.85), calls=%async_computation.3 | async-start | bytes 3145728 | tf_op jit(solution)/shard_map/all_to_all | solution.py:272
  143.8 0.6 fusion.refs_2_
  144.5 36.0 %all-to-all-done.3.refs_1_ = bf16[8,24,32,128]{3,2,1,0:T(8,128)(2,1)S(1)} async-done(((bf16[8,24,32,128]{3,2,1,0:T(8,128)(2,1)}), bf16[8,24,32,128]{3,2,1,0:T(8,128)(2,1)S(1)}, u32[]{:S(2)}, u32[]{:S(2)}) %all-to-all-start.3) | async-done | bytes 1572896 | tf_op jit(solution)/shard_map/all_to_all | solution.py:272
  180.5 0.0 copy-start.1
  180.5 1.1 copy-done.1
  181.6 10.6 %shard_map.86 = f32[4096,256]{1,0:T(8,128)} custom-call(bf16[8,8,32,128]{3,2,1,0:T(8,128)(2,1)} %all-to-all-done.1.refs_0_, bf16[8,24,32,128]{3,2,1,0:T(8,128)(2,1)} %copy-done.1, bf16[128,128]{1,0:T(8,128)(2,1)} %fusion.refs_2_), custom_call_target="tpu_custom_call" | custom-call | tf_op jit(solution)/shard_map/pallas_call | solution.py:249
Async XLA Ops:
  9.9 34.5 %all-to-all-start = ((bf16[32,2,8,1024]{3,2,1,0:T(8,128)(2,1)}), bf16[32,2,8,1024]{3,2,1,0:T(8,128)(2,1)S(1)}, u32[]{:S(2)}, u32[]{:S(2)}) async-start(bf16[32,2,8,1024]{3,2,1,0:T(8,128)(2,1)} %bitcast.7), calls=%async_computation | async-start | bytes 2097152 | tf_op jit(solution)/shard_map/all_to_all | solution.py:271
  44.4 1.0 copy-start.2
  45.4 75.3 %all-to-all-start.2 = ((bf16[32,2,24,1024]{3,2,1,0:T(8,128)(2,1)}), bf16[32,2,24,1024]{3,2,1,0:T(8,128)(2,1)S(1)}, u32[]{:S(2)}, u32[]{:S(2)}) async-start(bf16[32,2,24,1024]{3,2,1,0:T(8,128)(2,1)} %bitcast.6), calls=%async_computation.2 | async-start | bytes 6291456 | tf_op jit(solution)/shard_map/all_to_all | solution.py:271
  120.7 4.2 %copy-start = (bf16[32,2,24,1024]{3,2,1,0:T(8,128)(2,1)}, bf16[32,2,24,1024]{3,2,1,0:T(8,128)(2,1)S(1)}, u32[]{:S(2)}) copy-start(bf16[32,2,24,1024]{3,2,1,0:T(8,128)(2,1)S(1)} %all-to-all-done.2.got) | copy-start | bytes 9437188
  120.7 19.5 %all-to-all-start.1 = ((bf16[8,8,32,128]{3,2,1,0:T(8,128)(2,1)}), bf16[8,8,32,128]{3,2,1,0:T(8,128)(2,1)}, u32[]{:S(2)}, u32[]{:S(2)}) async-start(bf16[8,8,32,128]{3,2,1,0:T(8,128)(2,1)} %shard_map.83), calls=%async_computation.1 | async-start | bytes 1048576 | tf_op jit(solution)/shard_map/all_to_all | solution.py:272
  140.2 40.2 %all-to-all-start.3 = ((bf16[8,24,32,128]{3,2,1,0:T(8,128)(2,1)}), bf16[8,24,32,128]{3,2,1,0:T(8,128)(2,1)S(1)}, u32[]{:S(2)}, u32[]{:S(2)}) async-start(bf16[8,24,32,128]{3,2,1,0:T(8,128)(2,1)} %shard_map.85), calls=%async_computation.3 | async-start | bytes 3145728 | tf_op jit(solution)/shard_map/all_to_all | solution.py:272
  180.5 1.2 copy-start.1
